TPU v7x, 128 devices: a whole 4x4x4 slice. The times are simulated.
128 devices in a mesh: section: 8 (over y, core), edge: 16 (over z, x).
Axes of the slice: x: 4, y: 4, z: 4, core: 2. Of those that a mesh axis runs over, the one named last changes fastest.
Arguments:
- layer_nodes: bfloat16 [8, 2, 256, 512], P('section'), may hold values from -6 to 6
- layer_edges: bfloat16 [8, 2, 4096, 512], P('section', None, 'edge'), may hold values from -6 to 6
- top_nodes: bfloat16 [2, 256, 512], replicated, may hold values from -1.5 to 1.5
- top_edges: bfloat16 [2, 4096, 512], P(None, 'edge'), may hold values from -1.5 to 1.5
- tile_blocks: int32 [2, 32, 2], P(None, 'edge'), may hold values from 0 to 1
- senders: int32 [2, 4096], P(None, 'edge'), may hold values from 0 to 127
- receivers: int32 [2, 4096], P(None, 'edge'), may hold values from 0 to 127
- w_send: bfloat16 [8, 512, 512], P('section'), may hold values from -0.0625 to 0.0625
- w_recv: bfloat16 [8, 512, 512], P('section'), may hold values from -0.0625 to 0.0625
- w_edge: bfloat16 [8, 512, 512], P('section'), may hold values from -0.25 to 0.25
- w_msg: bfloat16 [8, 512, 512], P('section'), may hold values from -0.125 to 0.125
- w_node: bfloat16 [8, 512, 512], P('section'), may hold values from -0.25 to 0.25
- w_agg: bfloat16 [8, 512, 512], P('section'), may hold values from -0.25 to 0.25
- w_out: bfloat16 [8, 512, 512], P('section'), may hold values from -0.125 to 0.125
Outputs:
- node_grads: bfloat16 [8, 2, 256, 512], P('section', None, 'edge')
- edge_grads: bfloat16 [8, 2, 4096, 512], P('section', None, 'edge')
- g_send: float32 [8, 512, 512], P('section', 'edge')
- g_recv: float32 [8, 512, 512], P('section', 'edge')
- g_edge: float32 [8, 512, 512], P('section', 'edge')
- g_msg: float32 [8, 512, 512], P('section', 'edge')
- g_node: float32 [8, 512, 512], P('section', 'edge')
- g_agg: float32 [8, 512, 512], P('section', 'edge')
- g_out: float32 [8, 512, 512], P('section', 'edge')
All inputs are finite; a program needn't handle non-finite values.
Results may differ from a plain program's by a relative error of at most 0.029.
Values may be sent and summed in bfloat16 or wider, within the bound.
A program may use at most 64 MiB of HBM per device.

v0:
```python
import jax
import jax.numpy as jnp
from jax import lax
from jax.sharding import PartitionSpec as P

BLOCK = 128


def shifted(shard, axis, by):
    peers = lax.axis_size(axis)
    pairs = [(i, i + by) for i in range(peers) if 0 <= i + by < peers]
    return lax.ppermute(shard, axis, pairs)


def silu_slope(values):
    sigma = jax.nn.sigmoid(values)
    return sigma * (1.0 + values * (1.0 - sigma))


def matmul(left, right):
    return jnp.dot(left, right, preferred_element_type=jnp.float32)


def times_transposed(left, right):
    return lax.dot_general(
        left, right, (((1,), (1,)), ((), ())), preferred_element_type=jnp.float32
    )


def transposed_times(left, right):
    return lax.dot_general(
        left, right, (((0,), (0,)), ((), ())), preferred_element_type=jnp.float32
    )


def to_edges(values, block_hot, edge_hot):
    width = values.shape[1]
    grouped = values.reshape(block_hot.shape[1], -1, width)
    picked = jnp.einsum(
        "tb,bcd->tcd", block_hot, grouped, preferred_element_type=jnp.float32
    ).astype(jnp.bfloat16)
    spread = jnp.einsum("tec,tcd->ted", edge_hot, picked, preferred_element_type=jnp.float32)
    return spread.reshape(-1, width).astype(jnp.bfloat16)


def to_nodes(values, block_hot, edge_hot):
    width = values.shape[1]
    per_tile = jnp.einsum(
        "tec,ted->tcd",
        edge_hot,
        values.reshape(block_hot.shape[0], -1, width),
        preferred_element_type=jnp.float32,
    )
    summed = jnp.einsum(
        "tb,tcd->bcd", block_hot.astype(jnp.float32), per_tile, precision=lax.Precision.HIGHEST
    )
    return summed.reshape(-1, width)


def body(
    layer_nodes,
    layer_edges,
    top_nodes,
    top_edges,
    tile_blocks,
    senders,
    receivers,
    w_send,
    w_recv,
    w_edge,
    w_msg,
    w_node,
    w_agg,
    w_out,
):
    sections = lax.axis_size("section")
    section = lax.axis_index("section")
    groups = lax.axis_size("edge")
    member = lax.axis_index("edge")
    nodes_all = layer_nodes[0]
    edges_all = layer_edges[0]
    batches = nodes_all.shape[0]
    node_count = nodes_all.shape[1]
    width = nodes_all.shape[2]
    tile_count = tile_blocks.shape[1]
    tile_len = edges_all.shape[1] // tile_count
    block_count = node_count // BLOCK
    row_count = node_count // groups
    weight_send, weight_recv, weight_edge, weight_msg = (w_send[0], w_recv[0], w_edge[0], w_msg[0])
    weight_node, weight_agg, weight_out = (w_node[0], w_agg[0], w_out[0])
    lanes = jnp.arange(BLOCK, dtype=jnp.int32)
    slots = jnp.arange(block_count, dtype=jnp.int32)
    send_hot = (senders.reshape(batches, tile_count, tile_len)[..., None] == lanes).astype(
        jnp.bfloat16
    )
    recv_hot = (receivers.reshape(batches, tile_count, tile_len)[..., None] == lanes).astype(
        jnp.bfloat16
    )
    send_block = (tile_blocks[:, :, 0][..., None] == slots).astype(jnp.bfloat16)
    recv_block = (tile_blocks[:, :, 1][..., None] == slots).astype(jnp.bfloat16)

    def advance(moment, carry):
        node_in_grad, edge_in_grad, totals, node_record, edge_record = carry
        batch_raw = moment - (sections - 1 - section)
        valid = (batch_raw >= 0) & (batch_raw < batches)
        batch = jnp.clip(batch_raw, 0, batches - 1)
        feats = lax.dynamic_index_in_dim(nodes_all, batch, 0, keepdims=False)
        edge_feats = lax.dynamic_index_in_dim(edges_all, batch, 0, keepdims=False)
        send_tiles = lax.dynamic_index_in_dim(send_hot, batch, 0, keepdims=False)
        recv_tiles = lax.dynamic_index_in_dim(recv_hot, batch, 0, keepdims=False)
        send_blocks = lax.dynamic_index_in_dim(send_block, batch, 0, keepdims=False)
        recv_blocks = lax.dynamic_index_in_dim(recv_block, batch, 0, keepdims=False)
        top_node = lax.dynamic_index_in_dim(top_nodes, batch, 0, keepdims=False)
        top_edge = lax.dynamic_index_in_dim(top_edges, batch, 0, keepdims=False)
        is_last = section == sections - 1
        grad_nodes = jnp.where(is_last, top_node, node_in_grad)
        grad_edges = jnp.where(is_last, top_edge, edge_in_grad)
        send_feats = to_edges(feats, send_blocks, send_tiles)
        recv_feats = to_edges(feats, recv_blocks, recv_tiles)
        pre = (
            matmul(send_feats, weight_send)
            + matmul(recv_feats, weight_recv)
            + matmul(edge_feats, weight_edge)
        )
        act = jax.nn.silu(pre).astype(jnp.bfloat16)
        message = matmul(act, weight_msg).astype(jnp.bfloat16)
        partial_agg = to_nodes(message, recv_blocks, recv_tiles)
        aggregate = lax.psum(partial_agg, "edge")
        agg_b = aggregate.astype(jnp.bfloat16)
        node_pre = matmul(feats, weight_node) + matmul(agg_b, weight_agg)
        node_act = jax.nn.silu(node_pre).astype(jnp.bfloat16)
        node_delta = (times_transposed(grad_nodes, weight_out) * silu_slope(node_pre)).astype(
            jnp.bfloat16
        )
        agg_grad = times_transposed(node_delta, weight_agg).astype(jnp.bfloat16)
        node_term = times_transposed(node_delta, weight_node)
        agg_edges = to_edges(agg_grad, recv_blocks, recv_tiles)
        message_grad = (grad_edges.astype(jnp.float32) + agg_edges.astype(jnp.float32)).astype(
            jnp.bfloat16
        )
        edge_delta = (times_transposed(message_grad, weight_msg) * silu_slope(pre)).astype(
            jnp.bfloat16
        )
        edge_out = (
            grad_edges.astype(jnp.float32) + times_transposed(edge_delta, weight_edge)
        ).astype(jnp.bfloat16)
        send_grad = times_transposed(edge_delta, weight_send).astype(jnp.bfloat16)
        recv_grad = times_transposed(edge_delta, weight_recv).astype(jnp.bfloat16)
        partial_back = to_nodes(send_grad, send_blocks, send_tiles) + to_nodes(
            recv_grad, recv_blocks, recv_tiles
        )
        edge_terms = lax.psum(partial_back, "edge")
        node_out = (grad_nodes.astype(jnp.float32) + node_term + edge_terms).astype(jnp.bfloat16)
        fresh = (
            transposed_times(send_feats, edge_delta),
            transposed_times(recv_feats, edge_delta),
            transposed_times(edge_feats, edge_delta),
            transposed_times(act, message_grad),
            transposed_times(feats, node_delta),
            transposed_times(agg_b, node_delta),
            transposed_times(node_act, grad_nodes),
        )
        totals = tuple(
            (jnp.where(valid, before + extra, before) for before, extra in zip(totals, fresh))
        )
        own_out = lax.dynamic_slice_in_dim(node_out, member * row_count, row_count, 0)
        node_record = jnp.where(
            valid, lax.dynamic_update_index_in_dim(node_record, own_out, batch, 0), node_record
        )
        edge_record = jnp.where(
            valid, lax.dynamic_update_index_in_dim(edge_record, edge_out, batch, 0), edge_record
        )
        sent_nodes, sent_edges = shifted((node_out, edge_out), "section", -1)
        return (sent_nodes, sent_edges, totals, node_record, edge_record)

    hidden = weight_send.shape[1]
    square_in = jnp.zeros((width, hidden), jnp.float32)
    square_back = jnp.zeros((hidden, width), jnp.float32)
    start = (
        jnp.zeros((node_count, width), jnp.bfloat16),
        jnp.zeros(edges_all.shape[1:], jnp.bfloat16),
        (square_in, square_in, square_in, square_back, square_in, square_in, square_back),
        jnp.zeros((batches, row_count, width), jnp.bfloat16),
        jnp.zeros(edges_all.shape, jnp.bfloat16),
    )
    finished = lax.fori_loop(0, sections + batches - 1, advance, start)
    totals, node_record, edge_record = (finished[2], finished[3], finished[4])
    sum_send, sum_recv, sum_edge, sum_msg, sum_node, sum_agg, sum_out = totals
    sum_send, sum_recv, sum_edge, sum_msg = (
        lax.psum_scatter(sum_send, "edge", scatter_dimension=0, tiled=True),
        lax.psum_scatter(sum_recv, "edge", scatter_dimension=0, tiled=True),
        lax.psum_scatter(sum_edge, "edge", scatter_dimension=0, tiled=True),
        lax.psum_scatter(sum_msg, "edge", scatter_dimension=0, tiled=True),
    )
    sum_node = lax.dynamic_slice_in_dim(sum_node, member * (width // groups), width // groups, 0)
    sum_agg = lax.dynamic_slice_in_dim(sum_agg, member * (width // groups), width // groups, 0)
    sum_out = lax.dynamic_slice_in_dim(sum_out, member * (hidden // groups), hidden // groups, 0)
    return (
        node_record[None],
        edge_record[None],
        sum_send[None],
        sum_recv[None],
        sum_edge[None],
        sum_msg[None],
        sum_node[None],
        sum_agg[None],
        sum_out[None],
    )


def solution(mesh):
    in_specs = (
        P("section", None, None, None),
        P("section", None, "edge", None),
        P(),
        P(None, "edge", None),
        P(None, "edge", None),
        P(None, "edge"),
        P(None, "edge"),
        P("section", None, None),
        P("section", None, None),
        P("section", None, None),
        P("section", None, None),
        P("section", None, None),
        P("section", None, None),
        P("section", None, None),
    )
    out_specs = (
        P("section", None, "edge", None),
        P("section", None, "edge", None),
        P("section", "edge", None),
        P("section", "edge", None),
        P("section", "edge", None),
        P("section", "edge", None),
        P("section", "edge", None),
        P("section", "edge", None),
        P("section", "edge", None),
    )
    return jax.shard_map(body, mesh=mesh, in_specs=in_specs, out_specs=out_specs, check_vma=False)
```

profile of v0, /device:TPU:0, one launch (start us, length us, event | category | flops | bytes accessed | tf_op | source)
XLA Modules:
  0.0 2031.3 jit_solution(16253940211328947030)
XLA Ops:
  13.3 1701.8 %while.36 = (s32[]{:T(128)}, bf16[256,512]{1,0:T(8,128)(2,1)S(1)}, bf16[256,512]{1,0:T(8,128)(2,1)S(1)}, f32[512,512]{1,0:T(8,128)}, f32[512,512]{1,0:T(8,128)},...) while((s32[]{:T(128)}, bf16[256,512]{1,0:T(8,128)(2,1)S(1)}, ...), condition=%wide.region_3.4_spmd.clone, body=%wide.region_0.3_spmd.clone.sunk | while | flops 2910199808 | bytes 137546704 | solution.py:186
  21.1 81.4 %all-reduce.4 = bf16[256,512]{1,0:T(8,128)(2,1)S(1)} all-reduce(f32[256,512]{1,0:T(8,128)S(1)} %bitcast.271), channel_id=1, replica_groups=mesh['section'=8,'edge'=16] {'edge'}, use_global_device_ids=true, to_apply=%region_1.1 | all-reduce | flops 131072 | bytes 786432 | tf_op jit(solution)/shard_map/while/body/eval_jaxpr/psum | solution.py:128
  129.5 69.2 %all-reduce.3.cloned.1.call-done = f32[256,512]{1,0:T(8,128)} async-done(((f32[256,512]{1,0:T(8,128)}), f32[256,512]{1,0:T(8,128)}) %all-reduce.3.cloned.1.call-update) | async-done | bytes 524304 | tf_op jit(solution)/shard_map/while/body/eval_jaxpr/psum | solution.py:152
  211.4 77.6 %all-reduce.4 = bf16[256,512]{1,0:T(8,128)(2,1)S(1)} all-reduce(f32[256,512]{1,0:T(8,128)S(1)} %bitcast.271), channel_id=1, replica_groups=mesh['section'=8,'edge'=16] {'edge'}, use_global_device_ids=true, to_apply=%region_1.1 | all-reduce | flops 131072 | bytes 786432 | tf_op jit(solution)/shard_map/while/body/eval_jaxpr/psum | solution.py:128
  306.7 2.9 add_select_fusion.17
  314.9 2.6 add_select_fusion.20
  317.5 70.1 %all-reduce.3.cloned.1.call-done = f32[256,512]{1,0:T(8,128)} async-done(((f32[256,512]{1,0:T(8,128)}), f32[256,512]{1,0:T(8,128)}) %all-reduce.3.cloned.1.call-update) | async-done | bytes 524304 | tf_op jit(solution)/shard_map/while/body/eval_jaxpr/psum | solution.py:152
  400.3 77.6 %all-reduce.4 = bf16[256,512]{1,0:T(8,128)(2,1)S(1)} all-reduce(f32[256,512]{1,0:T(8,128)S(1)} %bitcast.271), channel_id=1, replica_groups=mesh['section'=8,'edge'=16] {'edge'}, use_global_device_ids=true, to_apply=%region_1.1 | all-reduce | flops 131072 | bytes 786432 | tf_op jit(solution)/shard_map/while/body/eval_jaxpr/psum | solution.py:128
  495.7 2.9 add_select_fusion.17
  506.5 70.1 %all-reduce.3.cloned.1.call-done = f32[256,512]{1,0:T(8,128)} async-done(((f32[256,512]{1,0:T(8,128)}), f32[256,512]{1,0:T(8,128)}) %all-reduce.3.cloned.1.call-update) | async-done | bytes 524304 | tf_op jit(solution)/shard_map/while/body/eval_jaxpr/psum | solution.py:152
  589.3 77.6 %all-reduce.4 = bf16[256,512]{1,0:T(8,128)(2,1)S(1)} all-reduce(f32[256,512]{1,0:T(8,128)S(1)} %bitcast.271), channel_id=1, replica_groups=mesh['section'=8,'edge'=16] {'edge'}, use_global_device_ids=true, to_apply=%region_1.1 | all-reduce | flops 131072 | bytes 786432 | tf_op jit(solution)/shard_map/while/body/eval_jaxpr/psum | solution.py:128
  684.6 2.9 add_select_fusion.17
  695.4 70.1 %all-reduce.3.cloned.1.call-done = f32[256,512]{1,0:T(8,128)} async-done(((f32[256,512]{1,0:T(8,128)}), f32[256,512]{1,0:T(8,128)}) %all-reduce.3.cloned.1.call-update) | async-done | bytes 524304 | tf_op jit(solution)/shard_map/while/body/eval_jaxpr/psum | solution.py:152
  778.2 77.6 %all-reduce.4 = bf16[256,512]{1,0:T(8,128)(2,1)S(1)} all-reduce(f32[256,512]{1,0:T(8,128)S(1)} %bitcast.271), channel_id=1, replica_groups=mesh['section'=8,'edge'=16] {'edge'}, use_global_device_ids=true, to_apply=%region_1.1 | all-reduce | flops 131072 | bytes 786432 | tf_op jit(solution)/shard_map/while/body/eval_jaxpr/psum | solution.py:128
  873.6 2.9 add_select_fusion.17
  884.4 70.1 %all-reduce.3.cloned.1.call-done = f32[256,512]{1,0:T(8,128)} async-done(((f32[256,512]{1,0:T(8,128)}), f32[256,512]{1,0:T(8,128)}) %all-reduce.3.cloned.1.call-update) | async-done | bytes 524304 | tf_op jit(solution)/shard_map/while/body/eval_jaxpr/psum | solution.py:152
  967.2 77.6 %all-reduce.4 = bf16[256,512]{1,0:T(8,128)(2,1)S(1)} all-reduce(f32[256,512]{1,0:T(8,128)S(1)} %bitcast.271), channel_id=1, replica_groups=mesh['section'=8,'edge'=16] {'edge'}, use_global_device_ids=true, to_apply=%region_1.1 | all-reduce | flops 131072 | bytes 786432 | tf_op jit(solution)/shard_map/while/body/eval_jaxpr/psum | solution.py:128
  1062.5 2.9 add_select_fusion.17
  1073.3 70.1 %all-reduce.3.cloned.1.call-done = f32[256,512]{1,0:T(8,128)} async-done(((f32[256,512]{1,0:T(8,128)}), f32[256,512]{1,0:T(8,128)}) %all-reduce.3.cloned.1.call-update) | async-done | bytes 524304 | tf_op jit(solution)/shard_map/while/body/eval_jaxpr/psum | solution.py:152
  1156.1 77.6 %all-reduce.4 = bf16[256,512]{1,0:T(8,128)(2,1)S(1)} all-reduce(f32[256,512]{1,0:T(8,128)S(1)} %bitcast.271), channel_id=1, replica_groups=mesh['section'=8,'edge'=16] {'edge'}, use_global_device_ids=true, to_apply=%region_1.1 | all-reduce | flops 131072 | bytes 786432 | tf_op jit(solution)/shard_map/while/body/eval_jaxpr/psum | solution.py:128
  1251.5 2.9 add_select_fusion.17
  1262.3 70.1 %all-reduce.3.cloned.1.call-done = f32[256,512]{1,0:T(8,128)} async-done(((f32[256,512]{1,0:T(8,128)}), f32[256,512]{1,0:T(8,128)}) %all-reduce.3.cloned.1.call-update) | async-done | bytes 524304 | tf_op jit(solution)/shard_map/while/body/eval_jaxpr/psum | solution.py:152
  1345.1 77.6 %all-reduce.4 = bf16[256,512]{1,0:T(8,128)(2,1)S(1)} all-reduce(f32[256,512]{1,0:T(8,128)S(1)} %bitcast.271), channel_id=1, replica_groups=mesh['section'=8,'edge'=16] {'edge'}, use_global_device_ids=true, to_apply=%region_1.1 | all-reduce | flops 131072 | bytes 786432 | tf_op jit(solution)/shard_map/while/body/eval_jaxpr/psum | solution.py:128
  1440.4 2.9 add_select_fusion.17
  1451.2 70.1 %all-reduce.3.cloned.1.call-done = f32[256,512]{1,0:T(8,128)} async-done(((f32[256,512]{1,0:T(8,128)}), f32[256,512]{1,0:T(8,128)}) %all-reduce.3.cloned.1.call-update) | async-done | bytes 524304 | tf_op jit(solution)/shard_map/while/body/eval_jaxpr/psum | solution.py:152
  1534.1 77.6 %all-reduce.4 = bf16[256,512]{1,0:T(8,128)(2,1)S(1)} all-reduce(f32[256,512]{1,0:T(8,128)S(1)} %bitcast.271), channel_id=1, replica_groups=mesh['section'=8,'edge'=16] {'edge'}, use_global_device_ids=true, to_apply=%region_1.1 | all-reduce | flops 131072 | bytes 786432 | tf_op jit(solution)/shard_map/while/body/eval_jaxpr/psum | solution.py:128
  1629.4 2.9 add_select_fusion.17
  1640.2 70.1 %all-reduce.3.cloned.1.call-done = f32[256,512]{1,0:T(8,128)} async-done(((f32[256,512]{1,0:T(8,128)}), f32[256,512]{1,0:T(8,128)}) %all-reduce.3.cloned.1.call-update) | async-done | bytes 524304 | tf_op jit(solution)/shard_map/while/body/eval_jaxpr/psum | solution.py:152
  1722.0 73.1 %reduce-scatter.5.cloned.1.call-done = f32[32,512]{1,0:T(8,128)} async-done(((f32[512,512]{1,0:T(8,128)}), f32[32,512]{1,0:T(8,128)}) %reduce-scatter.5.cloned.1.call-update) | async-done | bytes 65552 | tf_op jit(solution)/shard_map/reduce_scatter | solution.py:190
  1795.1 76.3 %reduce-scatter.7.cloned.1.call-done = f32[32,512]{1,0:T(8,128)} async-done(((f32[512,512]{1,0:T(8,128)}), f32[32,512]{1,0:T(8,128)}) %reduce-scatter.7.cloned.1.call-update) | async-done | bytes 65552 | tf_op jit(solution)/shard_map/reduce_scatter | solution.py:191
  1871.4 76.0 %reduce-scatter.9.cloned.1.call-done = f32[32,512]{1,0:T(8,128)} async-done(((f32[512,512]{1,0:T(8,128)}), f32[32,512]{1,0:T(8,128)}) %reduce-scatter.9.cloned.1.call-update) | async-done | bytes 65552 | tf_op jit(solution)/shard_map/reduce_scatter | solution.py:192
  1947.4 76.5 %reduce-scatter.11.cloned.1.call-done = f32[32,512]{1,0:T(8,128)} async-done(((f32[512,512]{1,0:T(8,128)}), f32[32,512]{1,0:T(8,128)}) %reduce-scatter.11.cloned.1.call-update) | async-done | bytes 65552 | tf_op jit(solution)/shard_map/reduce_scatter | solution.py:193
  (991 shorter events, 351.5 us)
Async XLA Ops:
  13.3 185.4 %all-reduce.3.cloned.1.call-start = ((), (), s32[]{:S(2)}) async-start(), calls=%async_computation.8 | async-start | bytes 1048576 | tf_op jit(solution)/shard_map/while/body/eval_jaxpr/psum | solution.py:152
  119.0 83.2 %collective-permute-start.1 = (bf16[256,512]{1,0:T(8,128)(2,1)}, bf16[256,512]{1,0:T(8,128)(2,1)S(1)}, u32[]{:S(2)}, u32[]{:S(2)}) collective-permute-start(bf16[256,512]{1,0:T(8,128)(2,1)} %get-tuple-element.1012), channel_id=1, source_target_pairs={{16,0},{32,16},{48,32},{64,48},{80,64},{96,80},{112,96},{17,1},{33... | collective-permute-start | bytes 786440 | tf_op jit(solution)/shard_map/while/body/eval_jaxpr/ppermute | solution.py:12
  200.1 3.4 collective-permute-start
  203.5 184.1 %all-reduce.3.cloned.1.call-start = ((), (), s32[]{:S(2)}) async-start(), calls=%async_computation.8 | async-start | bytes 1048576 | tf_op jit(solution)/shard_map/while/body/eval_jaxpr/psum | solution.py:152
  305.4 85.7 %collective-permute-start.1 = (bf16[256,512]{1,0:T(8,128)(2,1)}, bf16[256,512]{1,0:T(8,128)(2,1)S(1)}, u32[]{:S(2)}, u32[]{:S(2)}) collective-permute-start(bf16[256,512]{1,0:T(8,128)(2,1)} %get-tuple-element.1012), channel_id=1, source_target_pairs={{16,0},{32,16},{48,32},{64,48},{80,64},{96,80},{112,96},{17,1},{33... | collective-permute-start | bytes 786440 | tf_op jit(solution)/shard_map/while/body/eval_jaxpr/ppermute | solution.py:12
  317.5 72.8 %copy-start.11 = (f32[512,512]{1,0:T(8,128)S(1)}, f32[512,512]{1,0:T(8,128)}, u32[]{:S(2)}) copy-start(f32[512,512]{1,0:T(8,128)} %get-tuple-element.1052) | copy-start | bytes 3145732 | tf_op jit(solution)/shard_map/while
  389.0 3.4 collective-permute-start
  392.5 184.1 %all-reduce.3.cloned.1.call-start = ((), (), s32[]{:S(2)}) async-start(), calls=%async_computation.8 | async-start | bytes 1048576 | tf_op jit(solution)/shard_map/while/body/eval_jaxpr/psum | solution.py:152
  494.4 85.7 %collective-permute-start.1 = (bf16[256,512]{1,0:T(8,128)(2,1)}, bf16[256,512]{1,0:T(8,128)(2,1)S(1)}, u32[]{:S(2)}, u32[]{:S(2)}) collective-permute-start(bf16[256,512]{1,0:T(8,128)(2,1)} %get-tuple-element.1012), channel_id=1, source_target_pairs={{16,0},{32,16},{48,32},{64,48},{80,64},{96,80},{112,96},{17,1},{33... | collective-permute-start | bytes 786440 | tf_op jit(solution)/shard_map/while/body/eval_jaxpr/ppermute | solution.py:12
  578.0 3.4 collective-permute-start
  581.4 184.1 %all-reduce.3.cloned.1.call-start = ((), (), s32[]{:S(2)}) async-start(), calls=%async_computation.8 | async-start | bytes 1048576 | tf_op jit(solution)/shard_map/while/body/eval_jaxpr/psum | solution.py:152
  683.3 85.7 %collective-permute-start.1 = (bf16[256,512]{1,0:T(8,128)(2,1)}, bf16[256,512]{1,0:T(8,128)(2,1)S(1)}, u32[]{:S(2)}, u32[]{:S(2)}) collective-permute-start(bf16[256,512]{1,0:T(8,128)(2,1)} %get-tuple-element.1012), channel_id=1, source_target_pairs={{16,0},{32,16},{48,32},{64,48},{80,64},{96,80},{112,96},{17,1},{33... | collective-permute-start | bytes 786440 | tf_op jit(solution)/shard_map/while/body/eval_jaxpr/ppermute | solution.py:12
  766.9 3.4 collective-permute-start
  770.4 184.1 %all-reduce.3.cloned.1.call-start = ((), (), s32[]{:S(2)}) async-start(), calls=%async_computation.8 | async-start | bytes 1048576 | tf_op jit(solution)/shard_map/while/body/eval_jaxpr/psum | solution.py:152
  872.3 85.7 %collective-permute-start.1 = (bf16[256,512]{1,0:T(8,128)(2,1)}, bf16[256,512]{1,0:T(8,128)(2,1)S(1)}, u32[]{:S(2)}, u32[]{:S(2)}) collective-permute-start(bf16[256,512]{1,0:T(8,128)(2,1)} %get-tuple-element.1012), channel_id=1, source_target_pairs={{16,0},{32,16},{48,32},{64,48},{80,64},{96,80},{112,96},{17,1},{33... | collective-permute-start | bytes 786440 | tf_op jit(solution)/shard_map/while/body/eval_jaxpr/ppermute | solution.py:12
  955.9 3.4 collective-permute-start
  959.3 184.1 %all-reduce.3.cloned.1.call-start = ((), (), s32[]{:S(2)}) async-start(), calls=%async_computation.8 | async-start | bytes 1048576 | tf_op jit(solution)/shard_map/while/body/eval_jaxpr/psum | solution.py:152
  1061.2 85.7 %collective-permute-start.1 = (bf16[256,512]{1,0:T(8,128)(2,1)}, bf16[256,512]{1,0:T(8,128)(2,1)S(1)}, u32[]{:S(2)}, u32[]{:S(2)}) collective-permute-start(bf16[256,512]{1,0:T(8,128)(2,1)} %get-tuple-element.1012), channel_id=1, source_target_pairs={{16,0},{32,16},{48,32},{64,48},{80,64},{96,80},{112,96},{17,1},{33... | collective-permute-start | bytes 786440 | tf_op jit(solution)/shard_map/while/body/eval_jaxpr/ppermute | solution.py:12
  1144.8 3.4 collective-permute-start
  1148.3 184.1 %all-reduce.3.cloned.1.call-start = ((), (), s32[]{:S(2)}) async-start(), calls=%async_computation.8 | async-start | bytes 1048576 | tf_op jit(solution)/shard_map/while/body/eval_jaxpr/psum | solution.py:152
  1250.2 85.7 %collective-permute-start.1 = (bf16[256,512]{1,0:T(8,128)(2,1)}, bf16[256,512]{1,0:T(8,128)(2,1)S(1)}, u32[]{:S(2)}, u32[]{:S(2)}) collective-permute-start(bf16[256,512]{1,0:T(8,128)(2,1)} %get-tuple-element.1012), channel_id=1, source_target_pairs={{16,0},{32,16},{48,32},{64,48},{80,64},{96,80},{112,96},{17,1},{33... | collective-permute-start | bytes 786440 | tf_op jit(solution)/shard_map/while/body/eval_jaxpr/ppermute | solution.py:12
  1333.8 3.4 collective-permute-start
  1337.2 184.1 %all-reduce.3.cloned.1.call-start = ((), (), s32[]{:S(2)}) async-start(), calls=%async_computation.8 | async-start | bytes 1048576 | tf_op jit(solution)/shard_map/while/body/eval_jaxpr/psum | solution.py:152
  1439.1 85.7 %collective-permute-start.1 = (bf16[256,512]{1,0:T(8,128)(2,1)}, bf16[256,512]{1,0:T(8,128)(2,1)S(1)}, u32[]{:S(2)}, u32[]{:S(2)}) collective-permute-start(bf16[256,512]{1,0:T(8,128)(2,1)} %get-tuple-element.1012), channel_id=1, source_target_pairs={{16,0},{32,16},{48,32},{64,48},{80,64},{96,80},{112,96},{17,1},{33... | collective-permute-start | bytes 786440 | tf_op jit(solution)/shard_map/while/body/eval_jaxpr/ppermute | solution.py:12
  1522.7 3.4 collective-permute-start
  1526.2 184.1 %all-reduce.3.cloned.1.call-start = ((), (), s32[]{:S(2)}) async-start(), calls=%async_computation.8 | async-start | bytes 1048576 | tf_op jit(solution)/shard_map/while/body/eval_jaxpr/psum | solution.py:152
  1628.1 85.7 %collective-permute-start.1 = (bf16[256,512]{1,0:T(8,128)(2,1)}, bf16[256,512]{1,0:T(8,128)(2,1)S(1)}, u32[]{:S(2)}, u32[]{:S(2)}) collective-permute-start(bf16[256,512]{1,0:T(8,128)(2,1)} %get-tuple-element.1012), channel_id=1, source_target_pairs={{16,0},{32,16},{48,32},{64,48},{80,64},{96,80},{112,96},{17,1},{33... | collective-permute-start | bytes 786440 | tf_op jit(solution)/shard_map/while/body/eval_jaxpr/ppermute | solution.py:12
  1711.7 3.4 collective-permute-start
  1715.1 80.0 %reduce-scatter.5.cloned.1.call-start = ((), (), s32[]{:S(2)}) async-start(), calls=%async_computation.4 | async-start | bytes 1114112 | tf_op jit(solution)/shard_map/reduce_scatter | solution.py:190
  1715.7 155.7 %reduce-scatter.7.cloned.1.call-start = ((), (), s32[]{:S(2)}) async-start(), calls=%async_computation.5 | async-start | bytes 1114112 | tf_op jit(solution)/shard_map/reduce_scatter | solution.py:191
  1716.3 231.1 %reduce-scatter.9.cloned.1.call-start = ((), (), s32[]{:S(2)}) async-start(), calls=%async_computation.6 | async-start | bytes 1114112 | tf_op jit(solution)/shard_map/reduce_scatter | solution.py:192
  1716.9 307.1 %reduce-scatter.11.cloned.1.call-start = ((), (), s32[]{:S(2)}) async-start(), calls=%async_computation.7 | async-start | bytes 1114112 | tf_op jit(solution)/shard_map/reduce_scatter | solution.py:193
  (283 other events, 925.2 us)
Sparse Core Ops, SparseCore 0:
  115.9 82.6 all-reduce.2
  302.4 85.1 all-reduce.2
  491.3 85.1 all-reduce.2
  680.3 85.1 all-reduce.2
  869.2 85.1 all-reduce.2
  1058.2 85.1 all-reduce.2
  1247.1 85.1 all-reduce.2
  1436.1 85.1 all-reduce.2
  1625.0 85.1 all-reduce.2
Sparse Core Ops, SparseCore 1:
  1719.4 75.7 reduce-scatter.4
  1799.1 72.2 reduce-scatter.6
  1875.0 72.3 reduce-scatter.8
  1951.5 72.4 reduce-scatter.10
where the time goes:
time: 2040 us; the launch traced here: 2030 us
  waiting for transfers between devices  946 us (46%)
  blocking collectives  702 us (34%)
  matrix products  214 us (10%)
  local copies, waits for them, and re-layouts  123 us (6%)
  starting transfers between devices  23.3 us (1%)
    psum x9, blocking collectives, advance(): aggregate = lax.psum(partial_agg, 'edge')  702 us
    psum x9, waiting for transfers between devices, advance(): edge_terms = lax.psum(partial_back, 'edge')  630 us
    while x558, local copies, waits for them, and re-layouts  96.3 us
    reduce_scatter x1, waiting for transfers between devices, body(): lax.psum_scatter(sum_msg, 'edge', scatter_dimension=0, tiled=True)  76.5 us
    reduce_scatter x1, waiting for transfers between devices, body(): lax.psum_scatter(sum_recv, 'edge', scatter_dimension=0, tiled=True)  76.3 us
    reduce_scatter x1, waiting for transfers between devices, body(): lax.psum_scatter(sum_edge, 'edge', scatter_dimension=0, tiled=True)  76 us
    reduce_scatter x1, waiting for transfers between devices, body(): lax.psum_scatter(sum_send, 'edge', scatter_dimension=0, tiled=True)  73.1 us
    dot_general x63, matrix products, transposed_times(): lax.dot_general(left, right, (((0,), (0,)), ((), ())), preferred_element_...  70.9 us
  transfers between devices with their start and end apart: 31, of which 22 were waited for; matrix products, arithmetic and copies ran while one was open for 5% of the time, Pallas kernels for 0%

commit v1 on v0

--- a/solution.py
+++ b/solution.py
@@ -149,7 +149,7 @@
         partial_back = to_nodes(send_grad, send_blocks, send_tiles) + to_nodes(
             recv_grad, recv_blocks, recv_tiles
         )
-        edge_terms = lax.psum(partial_back, "edge")
+        edge_terms = jnp.sum(lax.all_gather(partial_back, "edge"), axis=0)
         node_out = (grad_nodes.astype(jnp.float32) + node_term + edge_terms).astype(jnp.bfloat16)
         fresh = (
             transposed_times(send_feats, edge_delta),

time: 2040 us -> 1950 us (0.956)
  waiting for transfers between devices: 946 us -> 782 us
  matrix products: 214 us -> 297 us
  local copies, waits for them, and re-layouts: 123 us -> 47.5 us
  other arithmetic: 2.35 us -> 64.2 us
    psum x9 -> x0, waiting for transfers between devices: 630 us -> none  [advance(): edge_terms = lax.psum(partial_back, 'edge')]
    all_gather x0 -> x9, waiting for transfers between devices: none -> 479 us  [advance(): edge_terms = jnp.sum(lax.all_gather(partial_back, 'edge'), axis=0)]
    while x558 -> x414, local copies, waits for them, and re-layouts: 96.3 us -> 20.1 us
    dot_general x63, matrix products: 70.9 us -> 123 us  [transposed_times(): lax.dot_general(left, right, (((0,), (0,)), ((), ())), preferred_element_...]
    reduce_sum x0 -> x9, other arithmetic: none -> 39.6 us  [advance(): edge_terms = jnp.sum(lax.all_gather(partial_back, 'edge'), axis=0)]
    dot_general x54, matrix products: 16.2 us -> 45.2 us  [matmul(): return jnp.dot(left, right, preferred_element_type=jnp.float32)]
  transfers between devices with their start and end apart: 31 -> 31, of which waited for: 22 -> 13; matrix products, arithmetic and copies ran while one was open for 5% -> 10% of each run, Pallas kernels for 0% -> 0%
where the time goes in v1:
time: 1950 us; the launch traced here: 1940 us
  waiting for transfers between devices  782 us (40%)
  blocking collectives  707 us (36%)
  matrix products  297 us (15%)
  other arithmetic  64.2 us (3%)
  local copies, waits for them, and re-layouts  47.5 us (2%)
  starting transfers between devices  24.5 us (1%)
    psum x9, blocking collectives, advance(): aggregate = lax.psum(partial_agg, 'edge')  707 us
    all_gather x9, waiting for transfers between devices, advance(): edge_terms = jnp.sum(lax.all_gather(partial_back, 'edge'), axis=0)  479 us
    dot_general x63, matrix products, transposed_times(): lax.dot_general(left, right, (((0,), (0,)), ((), ())), preferred_element_...  123 us
    reduce_scatter x1, waiting for transfers between devices, body(): lax.psum_scatter(sum_msg, 'edge', scatter_dimension=0, tiled=True)  76.5 us
    reduce_scatter x1, waiting for transfers between devices, body(): lax.psum_scatter(sum_recv, 'edge', scatter_dimension=0, tiled=True)  76.4 us
    reduce_scatter x1, waiting for transfers between devices, body(): lax.psum_scatter(sum_edge, 'edge', scatter_dimension=0, tiled=True)  76 us
    reduce_scatter x1, waiting for transfers between devices, body(): lax.psum_scatter(sum_send, 'edge', scatter_dimension=0, tiled=True)  71.8 us
    dot_general x63, matrix products, times_transposed(): lax.dot_general(left, right, (((1,), (1,)), ((), ())), preferred_element_...  49.7 us
  transfers between devices with their start and end apart: 31, of which 13 were waited for; matrix products, arithmetic and copies ran while one was open for 10% of the time, Pallas kernels for 0%

profile of v1, /device:TPU:0, one launch (start us, length us, event | category | flops | bytes accessed | tf_op | source)
XLA Modules:
  0.0 1941.8 jit_solution(3604530771544648667)
XLA Ops:
  13.5 1613.4 %while.36 = (s32[]{:T(128)}, bf16[256,512]{1,0:T(8,128)(2,1)}, bf16[256,512]{1,0:T(8,128)(2,1)S(1)}, f32[512,512]{1,0:T(8,128)}, f32[512,512]{1,0:T(8,128)}, /*i...) while((s32[]{:T(128)}, bf16[256,512]{1,0:T(8,128)(2,1)}, ...), condition=%wide.region_3.4_spmd.clone, body=%wide.region_0.3_spmd.clone.sunk | while | flops 2912428032 | bytes 141479168 | solution.py:186
  23.5 81.6 %all-reduce.1 = bf16[256,512]{1,0:T(8,128)(2,1)S(1)} all-reduce(f32[256,512]{1,0:T(8,128)S(1)} %bitcast.271), channel_id=1, replica_groups=mesh['section'=8,'edge'=16] {'edge'}, use_global_device_ids=true, to_apply=%region_1.1 | all-reduce | flops 131072 | bytes 786432 | tf_op jit(solution)/shard_map/while/body/eval_jaxpr/psum | solution.py:128
  127.3 57.1 %all-gather.2.cloned.1.call-done = f32[16,256,512]{2,1,0:T(8,128)} async-done(((f32[1,256,512]{2,1,0:T(8,128)}), f32[16,256,512]{2,1,0:T(8,128)}) %all-gather.2.cloned.1.call-update) | async-done | bytes 8388624 | tf_op jit(solution)/shard_map/while/body/eval_jaxpr/all_gather | solution.py:152
  184.5 4.4 reduce_sum.17
  204.8 78.2 %all-reduce.1 = bf16[256,512]{1,0:T(8,128)(2,1)S(1)} all-reduce(f32[256,512]{1,0:T(8,128)S(1)} %bitcast.271), channel_id=1, replica_groups=mesh['section'=8,'edge'=16] {'edge'}, use_global_device_ids=true, to_apply=%region_1.1 | all-reduce | flops 131072 | bytes 786432 | tf_op jit(solution)/shard_map/while/body/eval_jaxpr/psum | solution.py:128
  310.5 52.8 %all-gather.2.cloned.1.call-done = f32[16,256,512]{2,1,0:T(8,128)} async-done(((f32[1,256,512]{2,1,0:T(8,128)}), f32[16,256,512]{2,1,0:T(8,128)}) %all-gather.2.cloned.1.call-update) | async-done | bytes 8388624 | tf_op jit(solution)/shard_map/while/body/eval_jaxpr/all_gather | solution.py:152
  363.3 4.4 reduce_sum.17
  384.0 78.2 %all-reduce.1 = bf16[256,512]{1,0:T(8,128)(2,1)S(1)} all-reduce(f32[256,512]{1,0:T(8,128)S(1)} %bitcast.271), channel_id=1, replica_groups=mesh['section'=8,'edge'=16] {'edge'}, use_global_device_ids=true, to_apply=%region_1.1 | all-reduce | flops 131072 | bytes 786432 | tf_op jit(solution)/shard_map/while/body/eval_jaxpr/psum | solution.py:128
  489.6 52.7 %all-gather.2.cloned.1.call-done = f32[16,256,512]{2,1,0:T(8,128)} async-done(((f32[1,256,512]{2,1,0:T(8,128)}), f32[16,256,512]{2,1,0:T(8,128)}) %all-gather.2.cloned.1.call-update) | async-done | bytes 8388624 | tf_op jit(solution)/shard_map/while/body/eval_jaxpr/all_gather | solution.py:152
  542.3 4.4 reduce_sum.17
  563.0 78.1 %all-reduce.1 = bf16[256,512]{1,0:T(8,128)(2,1)S(1)} all-reduce(f32[256,512]{1,0:T(8,128)S(1)} %bitcast.271), channel_id=1, replica_groups=mesh['section'=8,'edge'=16] {'edge'}, use_global_device_ids=true, to_apply=%region_1.1 | all-reduce | flops 131072 | bytes 786432 | tf_op jit(solution)/shard_map/while/body/eval_jaxpr/psum | solution.py:128
  668.6 52.7 %all-gather.2.cloned.1.call-done = f32[16,256,512]{2,1,0:T(8,128)} async-done(((f32[1,256,512]{2,1,0:T(8,128)}), f32[16,256,512]{2,1,0:T(8,128)}) %all-gather.2.cloned.1.call-update) | async-done | bytes 8388624 | tf_op jit(solution)/shard_map/while/body/eval_jaxpr/all_gather | solution.py:152
  721.3 4.4 reduce_sum.17
  742.0 78.1 %all-reduce.1 = bf16[256,512]{1,0:T(8,128)(2,1)S(1)} all-reduce(f32[256,512]{1,0:T(8,128)S(1)} %bitcast.271), channel_id=1, replica_groups=mesh['section'=8,'edge'=16] {'edge'}, use_global_device_ids=true, to_apply=%region_1.1 | all-reduce | flops 131072 | bytes 786432 | tf_op jit(solution)/shard_map/while/body/eval_jaxpr/psum | solution.py:128
  847.6 52.7 %all-gather.2.cloned.1.call-done = f32[16,256,512]{2,1,0:T(8,128)} async-done(((f32[1,256,512]{2,1,0:T(8,128)}), f32[16,256,512]{2,1,0:T(8,128)}) %all-gather.2.cloned.1.call-update) | async-done | bytes 8388624 | tf_op jit(solution)/shard_map/while/body/eval_jaxpr/all_gather | solution.py:152
  900.3 4.4 reduce_sum.17
  921.0 78.2 %all-reduce.1 = bf16[256,512]{1,0:T(8,128)(2,1)S(1)} all-reduce(f32[256,512]{1,0:T(8,128)S(1)} %bitcast.271), channel_id=1, replica_groups=mesh['section'=8,'edge'=16] {'edge'}, use_global_device_ids=true, to_apply=%region_1.1 | all-reduce | flops 131072 | bytes 786432 | tf_op jit(solution)/shard_map/while/body/eval_jaxpr/psum | solution.py:128
  1026.6 52.7 %all-gather.2.cloned.1.call-done = f32[16,256,512]{2,1,0:T(8,128)} async-done(((f32[1,256,512]{2,1,0:T(8,128)}), f32[16,256,512]{2,1,0:T(8,128)}) %all-gather.2.cloned.1.call-update) | async-done | bytes 8388624 | tf_op jit(solution)/shard_map/while/body/eval_jaxpr/all_gather | solution.py:152
  1079.3 4.4 reduce_sum.17
  1100.0 78.1 %all-reduce.1 = bf16[256,512]{1,0:T(8,128)(2,1)S(1)} all-reduce(f32[256,512]{1,0:T(8,128)S(1)} %bitcast.271), channel_id=1, replica_groups=mesh['section'=8,'edge'=16] {'edge'}, use_global_device_ids=true, to_apply=%region_1.1 | all-reduce | flops 131072 | bytes 786432 | tf_op jit(solution)/shard_map/while/body/eval_jaxpr/psum | solution.py:128
  1205.5 52.7 %all-gather.2.cloned.1.call-done = f32[16,256,512]{2,1,0:T(8,128)} async-done(((f32[1,256,512]{2,1,0:T(8,128)}), f32[16,256,512]{2,1,0:T(8,128)}) %all-gather.2.cloned.1.call-update) | async-done | bytes 8388624 | tf_op jit(solution)/shard_map/while/body/eval_jaxpr/all_gather | solution.py:152
  1258.2 4.4 reduce_sum.17
  1278.9 78.1 %all-reduce.1 = bf16[256,512]{1,0:T(8,128)(2,1)S(1)} all-reduce(f32[256,512]{1,0:T(8,128)S(1)} %bitcast.271), channel_id=1, replica_groups=mesh['section'=8,'edge'=16] {'edge'}, use_global_device_ids=true, to_apply=%region_1.1 | all-reduce | flops 131072 | bytes 786432 | tf_op jit(solution)/shard_map/while/body/eval_jaxpr/psum | solution.py:128
  1384.5 52.7 %all-gather.2.cloned.1.call-done = f32[16,256,512]{2,1,0:T(8,128)} async-done(((f32[1,256,512]{2,1,0:T(8,128)}), f32[16,256,512]{2,1,0:T(8,128)}) %all-gather.2.cloned.1.call-update) | async-done | bytes 8388624 | tf_op jit(solution)/shard_map/while/body/eval_jaxpr/all_gather | solution.py:152
  1437.2 4.4 reduce_sum.17
  1457.9 78.2 %all-reduce.1 = bf16[256,512]{1,0:T(8,128)(2,1)S(1)} all-reduce(f32[256,512]{1,0:T(8,128)S(1)} %bitcast.271), channel_id=1, replica_groups=mesh['section'=8,'edge'=16] {'edge'}, use_global_device_ids=true, to_apply=%region_1.1 | all-reduce | flops 131072 | bytes 786432 | tf_op jit(solution)/shard_map/while/body/eval_jaxpr/psum | solution.py:128
  1563.5 52.7 %all-gather.2.cloned.1.call-done = f32[16,256,512]{2,1,0:T(8,128)} async-done(((f32[1,256,512]{2,1,0:T(8,128)}), f32[16,256,512]{2,1,0:T(8,128)}) %all-gather.2.cloned.1.call-update) | async-done | bytes 8388624 | tf_op jit(solution)/shard_map/while/body/eval_jaxpr/all_gather | solution.py:152
  1616.2 4.4 reduce_sum.17
  1633.8 71.8 %reduce-scatter.5.cloned.1.call-done = f32[32,512]{1,0:T(8,128)} async-done(((f32[512,512]{1,0:T(8,128)}), f32[32,512]{1,0:T(8,128)}) %reduce-scatter.5.cloned.1.call-update) | async-done | bytes 65552 | tf_op jit(solution)/shard_map/reduce_scatter | solution.py:190
  1705.7 76.4 %reduce-scatter.7.cloned.1.call-done = f32[32,512]{1,0:T(8,128)} async-done(((f32[512,512]{1,0:T(8,128)}), f32[32,512]{1,0:T(8,128)}) %reduce-scatter.7.cloned.1.call-update) | async-done | bytes 65552 | tf_op jit(solution)/shard_map/reduce_scatter | solution.py:191
  1782.0 76.0 %reduce-scatter.9.cloned.1.call-done = f32[32,512]{1,0:T(8,128)} async-done(((f32[512,512]{1,0:T(8,128)}), f32[32,512]{1,0:T(8,128)}) %reduce-scatter.9.cloned.1.call-update) | async-done | bytes 65552 | tf_op jit(solution)/shard_map/reduce_scatter | solution.py:192
  1858.0 76.5 %reduce-scatter.11.cloned.1.call-done = f32[32,512]{1,0:T(8,128)} async-done(((f32[512,512]{1,0:T(8,128)}), f32[32,512]{1,0:T(8,128)}) %reduce-scatter.11.cloned.1.call-update) | async-done | bytes 65552 | tf_op jit(solution)/shard_map/reduce_scatter | solution.py:193
  (846 shorter events, 395.7 us)
Async XLA Ops:
  13.5 170.9 %all-gather.2.cloned.1.call-start = ((), (), s32[]{:S(2)}) async-start(), calls=%async_computation.8 | async-start | bytes 8912896 | tf_op jit(solution)/shard_map/while/body/eval_jaxpr/all_gather | solution.py:152
  15.0 91.6 %copy-start.2 = (bf16[512,512]{1,0:T(8,128)(2,1)S(1)}, bf16[512,512]{1,0:T(8,128)(2,1)}, u32[]{:S(2)}) copy-start(bf16[512,512]{1,0:T(8,128)(2,1)} %get-tuple-element.1109) | copy-start | bytes 1572868 | tf_op jit(solution)/shard_map/while
  118.3 75.8 %collective-permute-start.1 = (bf16[256,512]{1,0:T(8,128)(2,1)}, bf16[256,512]{1,0:T(8,128)(2,1)S(1)}, u32[]{:S(2)}, u32[]{:S(2)}) collective-permute-start(bf16[256,512]{1,0:T(8,128)(2,1)} %get-tuple-element.1012), channel_id=1, source_target_pairs={{16,0},{32,16},{48,32},{64,48},{80,64},{96,80},{112,96},{17,1},{33... | collective-permute-start | bytes 786440 | tf_op jit(solution)/shard_map/while/body/eval_jaxpr/ppermute | solution.py:12
  189.3 4.9 collective-permute-start
  194.8 168.5 %all-gather.2.cloned.1.call-start = ((), (), s32[]{:S(2)}) async-start(), calls=%async_computation.8 | async-start | bytes 8912896 | tf_op jit(solution)/shard_map/while/body/eval_jaxpr/all_gather | solution.py:152
  296.2 77.1 %collective-permute-start.1 = (bf16[256,512]{1,0:T(8,128)(2,1)}, bf16[256,512]{1,0:T(8,128)(2,1)S(1)}, u32[]{:S(2)}, u32[]{:S(2)}) collective-permute-start(bf16[256,512]{1,0:T(8,128)(2,1)} %get-tuple-element.1012), channel_id=1, source_target_pairs={{16,0},{32,16},{48,32},{64,48},{80,64},{96,80},{112,96},{17,1},{33... | collective-permute-start | bytes 786440 | tf_op jit(solution)/shard_map/while/body/eval_jaxpr/ppermute | solution.py:12
  368.1 5.3 collective-permute-start
  374.0 168.3 %all-gather.2.cloned.1.call-start = ((), (), s32[]{:S(2)}) async-start(), calls=%async_computation.8 | async-start | bytes 8912896 | tf_op jit(solution)/shard_map/while/body/eval_jaxpr/all_gather | solution.py:152
  475.4 77.0 %collective-permute-start.1 = (bf16[256,512]{1,0:T(8,128)(2,1)}, bf16[256,512]{1,0:T(8,128)(2,1)S(1)}, u32[]{:S(2)}, u32[]{:S(2)}) collective-permute-start(bf16[256,512]{1,0:T(8,128)(2,1)} %get-tuple-element.1012), channel_id=1, source_target_pairs={{16,0},{32,16},{48,32},{64,48},{80,64},{96,80},{112,96},{17,1},{33... | collective-permute-start | bytes 786440 | tf_op jit(solution)/shard_map/while/body/eval_jaxpr/ppermute | solution.py:12
  547.1 5.3 collective-permute-start
  553.0 168.3 %all-gather.2.cloned.1.call-start = ((), (), s32[]{:S(2)}) async-start(), calls=%async_computation.8 | async-start | bytes 8912896 | tf_op jit(solution)/shard_map/while/body/eval_jaxpr/all_gather | solution.py:152
  654.4 76.9 %collective-permute-start.1 = (bf16[256,512]{1,0:T(8,128)(2,1)}, bf16[256,512]{1,0:T(8,128)(2,1)S(1)}, u32[]{:S(2)}, u32[]{:S(2)}) collective-permute-start(bf16[256,512]{1,0:T(8,128)(2,1)} %get-tuple-element.1012), channel_id=1, source_target_pairs={{16,0},{32,16},{48,32},{64,48},{80,64},{96,80},{112,96},{17,1},{33... | collective-permute-start | bytes 786440 | tf_op jit(solution)/shard_map/while/body/eval_jaxpr/ppermute | solution.py:12
  726.0 5.3 collective-permute-start
  732.0 168.3 %all-gather.2.cloned.1.call-start = ((), (), s32[]{:S(2)}) async-start(), calls=%async_computation.8 | async-start | bytes 8912896 | tf_op jit(solution)/shard_map/while/body/eval_jaxpr/all_gather | solution.py:152
  833.3 77.0 %collective-permute-start.1 = (bf16[256,512]{1,0:T(8,128)(2,1)}, bf16[256,512]{1,0:T(8,128)(2,1)S(1)}, u32[]{:S(2)}, u32[]{:S(2)}) collective-permute-start(bf16[256,512]{1,0:T(8,128)(2,1)} %get-tuple-element.1012), channel_id=1, source_target_pairs={{16,0},{32,16},{48,32},{64,48},{80,64},{96,80},{112,96},{17,1},{33... | collective-permute-start | bytes 786440 | tf_op jit(solution)/shard_map/while/body/eval_jaxpr/ppermute | solution.py:12
  905.0 5.3 collective-permute-start
  911.0 168.3 %all-gather.2.cloned.1.call-start = ((), (), s32[]{:S(2)}) async-start(), calls=%async_computation.8 | async-start | bytes 8912896 | tf_op jit(solution)/shard_map/while/body/eval_jaxpr/all_gather | solution.py:152
  1012.3 76.9 %collective-permute-start.1 = (bf16[256,512]{1,0:T(8,128)(2,1)}, bf16[256,512]{1,0:T(8,128)(2,1)S(1)}, u32[]{:S(2)}, u32[]{:S(2)}) collective-permute-start(bf16[256,512]{1,0:T(8,128)(2,1)} %get-tuple-element.1012), channel_id=1, source_target_pairs={{16,0},{32,16},{48,32},{64,48},{80,64},{96,80},{112,96},{17,1},{33... | collective-permute-start | bytes 786440 | tf_op jit(solution)/shard_map/while/body/eval_jaxpr/ppermute | solution.py:12
  1084.0 5.3 collective-permute-start
  1090.0 168.3 %all-gather.2.cloned.1.call-start = ((), (), s32[]{:S(2)}) async-start(), calls=%async_computation.8 | async-start | bytes 8912896 | tf_op jit(solution)/shard_map/while/body/eval_jaxpr/all_gather | solution.py:152
  1191.3 76.9 %collective-permute-start.1 = (bf16[256,512]{1,0:T(8,128)(2,1)}, bf16[256,512]{1,0:T(8,128)(2,1)S(1)}, u32[]{:S(2)}, u32[]{:S(2)}) collective-permute-start(bf16[256,512]{1,0:T(8,128)(2,1)} %get-tuple-element.1012), channel_id=1, source_target_pairs={{16,0},{32,16},{48,32},{64,48},{80,64},{96,80},{112,96},{17,1},{33... | collective-permute-start | bytes 786440 | tf_op jit(solution)/shard_map/while/body/eval_jaxpr/ppermute | solution.py:12
  1263.0 5.3 collective-permute-start
  1268.9 168.3 %all-gather.2.cloned.1.call-start = ((), (), s32[]{:S(2)}) async-start(), calls=%async_computation.8 | async-start | bytes 8912896 | tf_op jit(solution)/shard_map/while/body/eval_jaxpr/all_gather | solution.py:152
  1370.3 77.0 %collective-permute-start.1 = (bf16[256,512]{1,0:T(8,128)(2,1)}, bf16[256,512]{1,0:T(8,128)(2,1)S(1)}, u32[]{:S(2)}, u32[]{:S(2)}) collective-permute-start(bf16[256,512]{1,0:T(8,128)(2,1)} %get-tuple-element.1012), channel_id=1, source_target_pairs={{16,0},{32,16},{48,32},{64,48},{80,64},{96,80},{112,96},{17,1},{33... | collective-permute-start | bytes 786440 | tf_op jit(solution)/shard_map/while/body/eval_jaxpr/ppermute | solution.py:12
  1442.0 5.3 collective-permute-start
  1447.9 168.3 %all-gather.2.cloned.1.call-start = ((), (), s32[]{:S(2)}) async-start(), calls=%async_computation.8 | async-start | bytes 8912896 | tf_op jit(solution)/shard_map/while/body/eval_jaxpr/all_gather | solution.py:152
  1549.3 76.9 %collective-permute-start.1 = (bf16[256,512]{1,0:T(8,128)(2,1)}, bf16[256,512]{1,0:T(8,128)(2,1)S(1)}, u32[]{:S(2)}, u32[]{:S(2)}) collective-permute-start(bf16[256,512]{1,0:T(8,128)(2,1)} %get-tuple-element.1012), channel_id=1, source_target_pairs={{16,0},{32,16},{48,32},{64,48},{80,64},{96,80},{112,96},{17,1},{33... | collective-permute-start | bytes 786440 | tf_op jit(solution)/shard_map/while/body/eval_jaxpr/ppermute | solution.py:12
  1621.0 5.3 collective-permute-start
  1626.9 78.7 %reduce-scatter.5.cloned.1.call-start = ((), (), s32[]{:S(2)}) async-start(), calls=%async_computation.4 | async-start | bytes 1114112 | tf_op jit(solution)/shard_map/reduce_scatter | solution.py:190
  1627.5 154.5 %reduce-scatter.7.cloned.1.call-start = ((), (), s32[]{:S(2)}) async-start(), calls=%async_computation.5 | async-start | bytes 1114112 | tf_op jit(solution)/shard_map/reduce_scatter | solution.py:191
  1628.1 229.9 %reduce-scatter.9.cloned.1.call-start = ((), (), s32[]{:S(2)}) async-start(), calls=%async_computation.6 | async-start | bytes 1114112 | tf_op jit(solution)/shard_map/reduce_scatter | solution.py:192
  1628.7 305.8 %reduce-scatter.11.cloned.1.call-start = ((), (), s32[]{:S(2)}) async-start(), calls=%async_computation.7 | async-start | bytes 1114112 | tf_op jit(solution)/shard_map/reduce_scatter | solution.py:193
  (206 other events, 4256.9 us)
Sparse Core Ops, SparseCore 0:
  116.2 68.2 all-gather.1
  294.2 69.0 all-gather.1
  473.3 68.9 all-gather.1
  652.3 68.9 all-gather.1
  831.3 68.9 all-gather.1
  1010.3 68.9 all-gather.1
  1189.2 68.9 all-gather.1
  1368.2 68.9 all-gather.1
  1547.2 68.9 all-gather.1
Sparse Core Ops, SparseCore 1:
  1631.2 74.4 reduce-scatter.4
  1709.6 72.3 reduce-scatter.6
  1785.7 72.3 reduce-scatter.8
  1862.1 72.3 reduce-scatter.10
